TPU v7x, 32 devices: a whole 2x2x4 slice. The times are simulated.
32 devices in a mesh: groups: 2 (over y), seq: 8 (over z, x), chan: 2 (over core).
Axes of the slice: x: 2, y: 2, z: 4, core: 2. Of those that a mesh axis runs over, the one named last changes fastest.
Arguments:
- signal: bfloat16 [4096, 1024], P(('groups', 'seq'), 'chan'), parts along dimension 0, may hold values from -6 to 6
- tangent: bfloat16 [4096, 1024], P(('groups', 'seq'), 'chan'), parts along dimension 0, may hold values from -6 to 6
- gains: float32 [2, 1024], P(None, 'chan'), may hold values from 0.5 to 2
- convolution_kernel: bfloat16 [2, 3072, 2, 512], P(None, 'seq', None, 'chan'), may hold values from -0.109375 to 0.109375
- mixing_kernel: bfloat16 [2, 512, 1024], P(None, 'seq', 'chan'), may hold values from -0.25 to 0.25
Outputs:
- out_signal: bfloat16 [4096, 1024], P(('groups', 'seq'), 'chan'), parts along dimension 0
- out_tangent: bfloat16 [4096, 1024], P(('groups', 'seq'), 'chan'), parts along dimension 0
There are 2 independent parts, one for each index of `groups`. A program takes and returns all parts, laid end to end along the dimension named above; an argument that names none is the same for every part. Nothing has to cross between parts.
All inputs are finite; a program needn't handle non-finite values.
Results may differ from a plain program's by a relative error of at most 0.0063.
Values may be sent and summed in bfloat16 or wider, within the bound.
No kernel may reach another device: no remote copies, remote signals or barrier semaphores. Data moves between devices by JAX's collectives and lax.ppermute only.
A program may use at most 64 MiB of HBM per device.

v0:
```python
import jax
import jax.numpy as jnp
from jax import lax
from jax.sharding import PartitionSpec as P

LAYERS = 2


def from_behind(block, axis, distance):
    devices = range(lax.axis_size(axis))
    route = [(i - distance, i) for i in devices if i - distance in devices]
    return lax.ppermute(block, axis, route)


def delayed_rows(block, delay_offset, mover):
    rows = block.shape[1]
    whole, rest = divmod(delay_offset, rows)
    parts = []
    if rest:
        parts.append(mover(block[:, rows - rest :], whole + 1))
    parts.append(mover(block[:, : rows - rest], whole))
    return jnp.concatenate(parts, 1)


def on_device(signal, tangent, gains, convolution_kernel, mixing_kernel):
    rows = signal.shape[0]
    half = signal.shape[1]
    width = half * lax.axis_size("chan")
    branch = convolution_kernel.shape[3]
    base = rows * lax.axis_size("seq") // 16
    state = signal
    dstate = tangent

    def move_half(piece, by):
        return from_behind(piece, "seq", by)

    for layer_number in range(LAYERS):
        dilation_step = base * 2**layer_number
        xval = state.astype(jnp.float32)
        dxval = dstate.astype(jnp.float32)
        partial_value = jnp.stack([jnp.sum(xval * xval, axis=1), jnp.sum(xval * dxval, axis=1)], 0)
        totals = lax.psum(partial_value, "chan")
        mean_sq = (totals[0] / width)[:, None]
        mean_cross = (totals[1] / width)[:, None]
        scale = lax.rsqrt(mean_sq + 1e-05)
        gain = gains[layer_number][None, :]
        normed = (gain * xval * scale).astype(jnp.bfloat16)
        dnormed = (gain * (dxval * scale - xval * scale * scale * scale * mean_cross)).astype(
            jnp.bfloat16
        )
        paired = jnp.stack([normed, dnormed], 0)
        taps = jnp.stack(
            [
                paired,
                delayed_rows(paired, dilation_step, move_half),
                delayed_rows(paired, 2 * dilation_step, move_half),
            ],
            2,
        )
        stacked = lax.all_gather(taps, "chan", axis=3, tiled=True)
        left = stacked.reshape(2 * rows, 3 * width)
        conv_local = convolution_kernel[layer_number].reshape(
            convolution_kernel.shape[1], 2 * branch
        )
        conv_whole = lax.all_gather(conv_local, "seq", axis=0, tiled=True)
        full = jnp.dot(left, conv_whole, preferred_element_type=jnp.float32)
        filt, gate = (full[:rows, :branch], full[:rows, branch:])
        dfilt, dgate = (full[rows:, :branch], full[rows:, branch:])
        tanh_f = jnp.tanh(filt)
        sig_g = jax.nn.sigmoid(gate)
        gated = (tanh_f * sig_g).astype(jnp.bfloat16)
        dgated = (
            (1.0 - tanh_f * tanh_f) * sig_g * dfilt + tanh_f * sig_g * (1.0 - sig_g) * dgate
        ).astype(jnp.bfloat16)
        branch_all = lax.all_gather(jnp.concatenate([gated, dgated], 0), "chan", axis=1, tiled=True)
        mix_whole = lax.all_gather(mixing_kernel[layer_number], "seq", axis=0, tiled=True)
        mixed = jnp.dot(branch_all, mix_whole, preferred_element_type=jnp.float32)
        state = (xval + mixed[:rows]).astype(jnp.bfloat16)
        dstate = (dxval + mixed[rows:]).astype(jnp.bfloat16)
    return (state, dstate)


def solution(mesh):
    return jax.shard_map(
        on_device,
        mesh=mesh,
        in_specs=(
            P(("groups", "seq"), "chan"),
            P(("groups", "seq"), "chan"),
            P(None, "chan"),
            P(None, "seq", None, "chan"),
            P(None, "seq", "chan"),
        ),
        out_specs=(P(("groups", "seq"), "chan"), P(("groups", "seq"), "chan")),
        check_vma=False,
    )
```

profile of v0, /device:TPU:0, one launch (start us, length us, event | category | flops | bytes accessed | tf_op | source)
XLA Modules:
  0.0 246.1 jit_solution(518207839076454163)
XLA Ops:
  7.2 0.0 all-gather.7.cloned.1.call-start
  7.2 1.1 copy.13
  8.3 1.1 copy.14
  9.4 0.1 fusion.10
  9.5 2.6 %psum.14 = f32[2,256]{1,0:T(2,128)S(1)} all-reduce(f32[2,256]{1,0:T(2,128)S(1)} %pad_maximum_fusion.6), channel_id=1, replica_groups=mesh['groups'=2,'seq'=8,'chan'=2] {'chan'}, use_global_device_ids=true, to_apply=%region_2.0 | all-reduce | flops 512 | bytes 4096 | tf_op jit(solution)/shard_map/psum | solution.py:42
  12.1 0.8 fusion.58
  12.9 0.2 fusion.29
  13.1 0.1 fusion.53
  13.2 4.8 %collective-permute-start.2 = (bf16[2,256,512]{1,2,0:T(8,128)(2,1)S(1)}, bf16[2,256,512]{1,2,0:T(8,128)(2,1)S(1)}, u32[]{:S(2)}, u32[]{:S(2)}) collective-permute-start(bf16[2,256,512]{1,2,0:T(8,128)(2,1)S(1)} %get-tuple-element.23), channel_id=1, source_target_pairs={{0,2},{2,4},{4,6},{6,8},{8,10},{10,12},{12,14},{1,3},{3,5},{5,7},{... | collective-permute-start | bytes 1572872 | tf_op jit(solution)/shard_map/ppermute | solution.py:12
  18.0 0.1 fusion.32
  18.1 3.6 %collective-permute-start = (bf16[2,128,512]{1,2,0:T(8,128)(2,1)S(1)}, bf16[2,128,512]{1,2,0:T(8,128)(2,1)S(1)}, u32[]{:S(2)}, u32[]{:S(2)}) collective-permute-start(bf16[2,128,512]{1,2,0:T(8,128)(2,1)S(1)} %get-tuple-element.24), channel_id=1, source_target_pairs={{0,2},{2,4},{4,6},{6,8},{8,10},{10,12},{12,14},{1,3},{3,5},{5,7},{... | collective-permute-start | bytes 786440 | tf_op jit(solution)/shard_map/ppermute | solution.py:12
  21.7 13.4 %collective-permute-done = bf16[2,128,512]{1,2,0:T(8,128)(2,1)S(1)} collective-permute-done((bf16[2,128,512]{1,2,0:T(8,128)(2,1)S(1)}, bf16[2,128,512]{1,2,0:T(8,128)(2,1)S(1)}, u32[]{:S(2)}, u32[]{:S(2)}) %collective-permute-start) | collective-permute-done | bytes 262176 | tf_op jit(solution)/shard_map/ppermute | solution.py:12
  35.1 0.1 maximum_bitcast_fusion
  35.2 1.3 pad_maximum_fusion
  36.5 0.0 all-gather.9.cloned.1.call-start
  36.6 0.5 fusion.56
  37.1 0.9 copy.23
  38.0 0.0 all-gather.11.cloned.1.call-start
  38.1 34.5 %all-gather = bf16[1,512,512]{2,1,0:T(8,128)(2,1)S(1)} all-gather(bf16[1,64,512]{2,1,0:T(8,128)(2,1)S(1)} %get-tuple-element.31), channel_id=2, replica_groups=mesh['groups'=2,'seq'=8,'chan'=2] {'seq'}, dimensions={1}, use_global_device_ids=true | all-gather | bytes 589824 | tf_op jit(solution)/shard_map/all_gather | solution.py:76
  72.6 5.1 %copy.15 = bf16[2,256,3,1024]{1,0,3,2:T(2,128)(2,1)S(1)} copy(bf16[2,256,3,1024]{1,3,0,2:T(8,128)(2,1)} %all-gather.7.cloned.1.call-done) | data formatting | bytes 6291456 | tf_op jit(solution)/shard_map/all_gather | solution.py:60
  77.7 2.2 copy.22
  79.9 35.4 %all-gather.9.cloned.1.call-done = bf16[3072,512]{1,0:T(8,128)(2,1)} async-done(((bf16[384,512]{1,0:T(8,128)(2,1)}), bf16[3072,512]{1,0:T(8,128)(2,1)}) %all-gather.9.cloned.1.call-update) | async-done | bytes 3145744 | tf_op jit(solution)/shard_map/all_gather | solution.py:65
  115.4 4.6 %fusion.59 = f32[512,512]{1,0:T(8,128)S(1)} fusion(bf16[512,3072]{0,1:T(8,128)(2,1)} %bitcast.57, bf16[3072,512]{1,0:T(8,128)(2,1)} %all-gather.9.cloned.1.call-done), kind=kOutput, calls=%fused_computation.96 | convolution fusion | flops 1610612736 | bytes 7340032 | tf_op jit(solution)/shard_map/dot_general | solution.py:66
  120.0 0.1 fusion.47
  120.2 2.2 all_gather.26
  122.4 0.5 fusion.26
  122.9 0.2 fusion.18
  123.0 2.5 %psum.15 = f32[2,256]{1,0:T(2,128)S(1)} all-reduce(f32[2,256]{1,0:T(2,128)S(1)} %pad_maximum_fusion.7), channel_id=1, replica_groups=mesh['groups'=2,'seq'=8,'chan'=2] {'chan'}, use_global_device_ids=true, to_apply=%region_5.0 | all-reduce | flops 512 | bytes 4096 | tf_op jit(solution)/shard_map/psum | solution.py:42
  125.5 0.2 fusion.28
  125.8 0.1 fusion.52
  125.8 2.5 %collective-permute-start.3 = (bf16[2,256,512]{1,2,0:T(8,128)(2,1)S(1)}, bf16[2,256,512]{1,2,0:T(8,128)(2,1)S(1)}, u32[]{:S(2)}, u32[]{:S(2)}) collective-permute-start(bf16[2,256,512]{1,2,0:T(8,128)(2,1)S(1)} %get-tuple-element.21), channel_id=1, source_target_pairs={{0,2},{2,4},{4,6},{6,8},{8,10},{10,12},{12,14},{1,3},{3,5},{5,7},{... | collective-permute-start | bytes 1572872 | tf_op jit(solution)/shard_map/ppermute | solution.py:12
  128.4 3.3 %collective-permute-start.4 = (bf16[2,256,512]{1,2,0:T(8,128)(2,1)S(1)}, bf16[2,256,512]{1,2,0:T(8,128)(2,1)S(1)}, u32[]{:S(2)}, u32[]{:S(2)}) collective-permute-start(bf16[2,256,512]{1,2,0:T(8,128)(2,1)S(1)} %get-tuple-element.21), channel_id=1, source_target_pairs={{0,4},{2,6},{4,8},{6,10},{8,12},{10,14},{1,5},{3,7},{5,9},{7,11},{... | collective-permute-start | bytes 1572872 | tf_op jit(solution)/shard_map/ppermute | solution.py:12
  131.7 8.1 %collective-permute-done.3 = bf16[2,256,512]{1,2,0:T(8,128)(2,1)S(1)} collective-permute-done((bf16[2,256,512]{1,2,0:T(8,128)(2,1)S(1)}, bf16[2,256,512]{1,2,0:T(8,128)(2,1)S(1)}, u32[]{:S(2)}, u32[]{:S(2)}) %collective-permute-start.3) | collective-permute-done | bytes 524320 | tf_op jit(solution)/shard_map/ppermute | solution.py:12
  139.8 3.1 %collective-permute-done.4 = bf16[2,256,512]{1,2,0:T(8,128)(2,1)S(1)} collective-permute-done((bf16[2,256,512]{1,2,0:T(8,128)(2,1)S(1)}, bf16[2,256,512]{1,2,0:T(8,128)(2,1)S(1)}, u32[]{:S(2)}, u32[]{:S(2)}) %collective-permute-start.4) | collective-permute-done | bytes 524320 | tf_op jit(solution)/shard_map/ppermute | solution.py:12
  142.9 1.3 pad_maximum_fusion.1
  144.2 0.0 all-gather.13.cloned.1.call-start
  144.3 0.9 copy.25
  145.2 40.1 %all-gather.1 = bf16[1,512,512]{2,1,0:T(8,128)(2,1)S(1)} all-gather(bf16[1,64,512]{2,1,0:T(8,128)(2,1)S(1)} %get-tuple-element.30), channel_id=3, replica_groups=mesh['groups'=2,'seq'=8,'chan'=2] {'seq'}, dimensions={1}, use_global_device_ids=true | all-gather | bytes 589824 | tf_op jit(solution)/shard_map/all_gather | solution.py:76
  185.3 5.1 %copy.16 = bf16[2,256,3,1024]{1,0,3,2:T(2,128)(2,1)S(1)} copy(bf16[2,256,3,1024]{1,3,0,2:T(8,128)(2,1)} %all-gather.11.cloned.1.call-done) | data formatting | bytes 6291456 | tf_op jit(solution)/shard_map/all_gather | solution.py:60
  190.4 2.2 copy.24
  192.7 37.5 %all-gather.13.cloned.1.call-done = bf16[3072,512]{1,0:T(8,128)(2,1)} async-done(((bf16[384,512]{1,0:T(8,128)(2,1)}), bf16[3072,512]{1,0:T(8,128)(2,1)}) %all-gather.13.cloned.1.call-update) | async-done | bytes 3145744 | tf_op jit(solution)/shard_map/all_gather | solution.py:65
  230.2 4.6 %fusion.60 = f32[512,512]{1,0:T(8,128)S(1)} fusion(bf16[512,3072]{0,1:T(8,128)(2,1)} %bitcast.58, bf16[3072,512]{1,0:T(8,128)(2,1)} %all-gather.13.cloned.1.call-done), kind=kOutput, calls=%fused_computation.97 | convolution fusion | flops 1610612736 | bytes 7340032 | tf_op jit(solution)/shard_map/dot_general | solution.py:66
  234.9 0.1 fusion.46
  235.1 2.2 all_gather.30
  237.2 0.5 fusion.24
  237.7 0.1 fusion.7
  237.8 0.8 copy.19
  238.7 0.8 copy.20
  (20 shorter events, 0.2 us)
Async XLA Ops:
  7.2 65.4 %all-gather.7.cloned.1.call-start = ((), (), s32[]{:S(2)}) async-start(), calls=%async_computation | async-start | bytes 4718592 | tf_op jit(solution)/shard_map/all_gather | solution.py:60
  13.2 21.9 %collective-permute-start.2 = (bf16[2,256,512]{1,2,0:T(8,128)(2,1)S(1)}, bf16[2,256,512]{1,2,0:T(8,128)(2,1)S(1)}, u32[]{:S(2)}, u32[]{:S(2)}) collective-permute-start(bf16[2,256,512]{1,2,0:T(8,128)(2,1)S(1)} %get-tuple-element.23), channel_id=1, source_target_pairs={{0,2},{2,4},{4,6},{6,8},{8,10},{10,12},{12,14},{1,3},{3,5},{5,7},{... | collective-permute-start | bytes 1572872 | tf_op jit(solution)/shard_map/ppermute | solution.py:12
  18.1 18.5 %copy-start = (bf16[2,384,2,256]{3,2,1,0:T(2,128)(2,1)S(1)}, bf16[2,384,2,256]{3,2,1,0:T(2,128)(2,1)}, u32[]{:S(2)}) copy-start(bf16[2,384,2,256]{3,2,1,0:T(2,128)(2,1)} %param.8) | copy-start | bytes 2359300
  18.1 17.0 %collective-permute-start = (bf16[2,128,512]{1,2,0:T(8,128)(2,1)S(1)}, bf16[2,128,512]{1,2,0:T(8,128)(2,1)S(1)}, u32[]{:S(2)}, u32[]{:S(2)}) collective-permute-start(bf16[2,128,512]{1,2,0:T(8,128)(2,1)S(1)} %get-tuple-element.24), channel_id=1, source_target_pairs={{0,2},{2,4},{4,6},{6,8},{8,10},{10,12},{12,14},{1,3},{3,5},{5,7},{... | collective-permute-start | bytes 786440 | tf_op jit(solution)/shard_map/ppermute | solution.py:12
  21.6 13.4 %collective-permute-start.1 = (bf16[2,128,512]{1,2,0:T(8,128)(2,1)S(1)}, bf16[2,128,512]{1,2,0:T(8,128)(2,1)S(1)}, u32[]{:S(2)}, u32[]{:S(2)}) collective-permute-start(bf16[2,128,512]{1,2,0:T(8,128)(2,1)S(1)} %get-tuple-element.25), channel_id=1, source_target_pairs={{0,0},{2,2},{4,4},{6,6},{8,8},{10,10},{12,12},{14,14},{1,1},{3,3},... | collective-permute-start | bytes 786440 | tf_op jit(solution)/shard_map/ppermute | solution.py:12
  35.1 2.9 %copy-start.1 = (bf16[2,64,512]{2,1,0:T(8,128)(2,1)S(1)}, bf16[2,64,512]{2,1,0:T(8,128)(2,1)}, u32[]{:S(2)}) copy-start(bf16[2,64,512]{2,1,0:T(8,128)(2,1)} %param.9) | copy-start | bytes 393220
  36.5 78.9 %all-gather.9.cloned.1.call-start = ((), (), s32[]{:S(2)}) async-start(), calls=%async_computation.1 | async-start | bytes 3538944 | tf_op jit(solution)/shard_map/all_gather | solution.py:65
  38.0 147.3 %all-gather.11.cloned.1.call-start = ((), (), s32[]{:S(2)}) async-start(), calls=%async_computation.2 | async-start | bytes 4718592 | tf_op jit(solution)/shard_map/all_gather | solution.py:60
  125.8 14.0 %collective-permute-start.3 = (bf16[2,256,512]{1,2,0:T(8,128)(2,1)S(1)}, bf16[2,256,512]{1,2,0:T(8,128)(2,1)S(1)}, u32[]{:S(2)}, u32[]{:S(2)}) collective-permute-start(bf16[2,256,512]{1,2,0:T(8,128)(2,1)S(1)} %get-tuple-element.21), channel_id=1, source_target_pairs={{0,2},{2,4},{4,6},{6,8},{8,10},{10,12},{12,14},{1,3},{3,5},{5,7},{... | collective-permute-start | bytes 1572872 | tf_op jit(solution)/shard_map/ppermute | solution.py:12
  128.4 14.5 %collective-permute-start.4 = (bf16[2,256,512]{1,2,0:T(8,128)(2,1)S(1)}, bf16[2,256,512]{1,2,0:T(8,128)(2,1)S(1)}, u32[]{:S(2)}, u32[]{:S(2)}) collective-permute-start(bf16[2,256,512]{1,2,0:T(8,128)(2,1)S(1)} %get-tuple-element.21), channel_id=1, source_target_pairs={{0,4},{2,6},{4,8},{6,10},{8,12},{10,14},{1,5},{3,7},{5,9},{7,11},{... | collective-permute-start | bytes 1572872 | tf_op jit(solution)/shard_map/ppermute | solution.py:12
  144.2 86.0 %all-gather.13.cloned.1.call-start = ((), (), s32[]{:S(2)}) async-start(), calls=%async_computation.3 | async-start | bytes 3538944 | tf_op jit(solution)/shard_map/all_gather | solution.py:65
Sparse Core Ops, SparseCore 0:
  36.6 14.3 all-gather.6
  53.2 62.1 all-gather.8
  144.4 21.7 all-gather.10
  168.2 62.0 all-gather.12
where the time goes:
time: 247 us; the launch traced here: 246 us
  waiting for transfers between devices  97.6 us (40%)
  blocking collectives  84 us (34%)
  local copies, waits for them, and re-layouts  21.7 us (9%)
  starting transfers between devices  14.4 us (6%)
  between operations  14 us (6%)
  matrix products  10.3 us (4%)
  other arithmetic  4.16 us (2%)
    all_gather x2, blocking collectives, on_device(): lax.all_gather(mixing_kernel[layer_number], 'seq', axis=0, tiled=True)  74.6 us
    all_gather x2, waiting for transfers between devices, on_device(): conv_whole = lax.all_gather(conv_local, 'seq', axis=0, tiled=True)  73 us
    ppermute x5, waiting for transfers between devices, from_behind(): return lax.ppermute(block, axis, route)  24.6 us
    ppermute x5, starting transfers between devices, from_behind(): return lax.ppermute(block, axis, route)  14.2 us
    all_gather x2, local copies, waits for them, and re-layouts, on_device(): stacked = lax.all_gather(taps, 'chan', axis=3, tiled=True)  10.3 us
    unnamed x12, local copies, waits for them, and re-layouts  10.1 us
    dot_general x2, matrix products, on_device(): full = jnp.dot(left, conv_whole, preferred_element_type=jnp.float32)  9.3 us
    psum x2, blocking collectives, on_device(): totals = lax.psum(partial_value, 'chan')  5.06 us
  transfers between devices with their start and end apart: 9, of which 5 were waited for; matrix products, arithmetic and copies ran while one was open for 7% of the time, Pallas kernels for 0%

commit v1 on v0

--- a/solution.py
+++ b/solution.py
@@ -1,9 +1,20 @@
+import functools
 import jax
 import jax.numpy as jnp
 from jax import lax
 from jax.sharding import PartitionSpec as P
+from jax.lax import all_gather
 
 LAYERS = 2
+
+
+def clear_pools(content, mesh_ax):
+    piece_out = all_gather(content, axis_name=mesh_ax)
+    main = jnp.sum(piece_out, axis=0)
+    return main
+
+
+direct_streams = functools.partial(clear_pools, mesh_ax="chan")
 
 
 def from_behind(block, axis, distance):
@@ -39,7 +50,7 @@
         xval = state.astype(jnp.float32)
         dxval = dstate.astype(jnp.float32)
         partial_value = jnp.stack([jnp.sum(xval * xval, axis=1), jnp.sum(xval * dxval, axis=1)], 0)
-        totals = lax.psum(partial_value, "chan")
+        totals = direct_streams(partial_value)
         mean_sq = (totals[0] / width)[:, None]
         mean_cross = (totals[1] / width)[:, None]
         scale = lax.rsqrt(mean_sq + 1e-05)

time: 247 us -> 245 us (level)
    psum x2 -> x0, blocking collectives: 5.06 us -> none  [on_device(): totals = lax.psum(partial_value, 'chan')]
    all_gather x0 -> x2, blocking collectives: none -> 3.71 us  [clear_pools(): piece_out = all_gather(content, axis_name=mesh_ax)]
    all_gather x2, blocking collectives: 74.6 us -> 77.1 us  [on_device(): lax.all_gather(mixing_kernel[layer_number], 'seq', axis=0, tiled=True)]
    unnamed x12 -> x18, local copies, waits for them, and re-layouts: 10.1 us -> 8.5 us
  transfers between devices with their start and end apart: 9 -> 9, of which waited for: 5 -> 5; matrix products, arithmetic and copies ran while one was open for 7% -> 6% of each run, Pallas kernels for 0% -> 0%
where the time goes in v1:
time: 245 us; the launch traced here: 244 us
  waiting for transfers between devices  96.9 us (40%)
  blocking collectives  85.2 us (35%)
  local copies, waits for them, and re-layouts  20.1 us (8%)
  starting transfers between devices  14.3 us (6%)
  between operations  14 us (6%)
  matrix products  9.37 us (4%)
  other arithmetic  4.19 us (2%)
    all_gather x2, blocking collectives, on_device(): lax.all_gather(mixing_kernel[layer_number], 'seq', axis=0, tiled=True)  77.1 us
    all_gather x2, waiting for transfers between devices, on_device(): conv_whole = lax.all_gather(conv_local, 'seq', axis=0, tiled=True)  72.2 us
    ppermute x5, waiting for transfers between devices, from_behind(): return lax.ppermute(block, axis, route)  24.7 us
    ppermute x5, starting transfers between devices, from_behind(): return lax.ppermute(block, axis, route)  14.2 us
    all_gather x2, local copies, waits for them, and re-layouts, on_device(): stacked = lax.all_gather(taps, 'chan', axis=3, tiled=True)  10.3 us
    unnamed x18, local copies, waits for them, and re-layouts  8.5 us
    dot_general x2, matrix products, on_device(): full = jnp.dot(left, conv_whole, preferred_element_type=jnp.float32)  8.4 us
  transfers between devices with their start and end apart: 9, of which 5 were waited for; matrix products, arithmetic and copies ran while one was open for 6% of the time, Pallas kernels for 0%

profile of v1, /device:TPU:0, one launch (start us, length us, event | category | flops | bytes accessed | tf_op | source)
XLA Modules:
  0.0 244.1 jit_solution(14915733902010601634)
XLA Ops:
  7.2 0.0 all-gather.11.cloned.1.call-start
  7.2 1.1 copy.21
  8.3 1.1 copy.22
  9.4 0.1 fusion.10
  9.5 1.9 all-gather.4
  11.5 0.8 fusion.58
  12.3 0.2 fusion.29
  12.5 0.1 fusion.53
  12.6 4.7 %collective-permute-start.2 = (bf16[2,256,512]{1,2,0:T(8,128)(2,1)S(1)}, bf16[2,256,512]{1,2,0:T(8,128)(2,1)S(1)}, u32[]{:S(2)}, u32[]{:S(2)}) collective-permute-start(bf16[2,256,512]{1,2,0:T(8,128)(2,1)S(1)} %get-tuple-element.25), channel_id=1, source_target_pairs={{0,2},{2,4},{4,6},{6,8},{8,10},{10,12},{12,14},{1,3},{3,5},{5,7},{... | collective-permute-start | bytes 1572872 | tf_op jit(solution)/shard_map/ppermute | solution.py:23
  17.3 0.1 fusion.32
  17.4 3.6 %collective-permute-start = (bf16[2,128,512]{1,2,0:T(8,128)(2,1)S(1)}, bf16[2,128,512]{1,2,0:T(8,128)(2,1)S(1)}, u32[]{:S(2)}, u32[]{:S(2)}) collective-permute-start(bf16[2,128,512]{1,2,0:T(8,128)(2,1)S(1)} %get-tuple-element.26), channel_id=1, source_target_pairs={{0,2},{2,4},{4,6},{6,8},{8,10},{10,12},{12,14},{1,3},{3,5},{5,7},{... | collective-permute-start | bytes 786440 | tf_op jit(solution)/shard_map/ppermute | solution.py:23
  21.0 13.4 %collective-permute-done = bf16[2,128,512]{1,2,0:T(8,128)(2,1)S(1)} collective-permute-done((bf16[2,128,512]{1,2,0:T(8,128)(2,1)S(1)}, bf16[2,128,512]{1,2,0:T(8,128)(2,1)S(1)}, u32[]{:S(2)}, u32[]{:S(2)}) %collective-permute-start) | collective-permute-done | bytes 262176 | tf_op jit(solution)/shard_map/ppermute | solution.py:23
  34.4 0.1 maximum_bitcast_fusion
  34.5 1.3 pad_maximum_fusion
  35.9 0.0 all-gather.13.cloned.1.call-start
  35.9 0.5 fusion.56
  36.5 0.9 copy.31
  37.4 0.0 all-gather.15.cloned.1.call-start
  37.4 34.5 %all-gather.1 = bf16[1,512,512]{2,1,0:T(8,128)(2,1)S(1)} all-gather(bf16[1,64,512]{2,1,0:T(8,128)(2,1)S(1)} %get-tuple-element.33), channel_id=3, replica_groups=mesh['groups'=2,'seq'=8,'chan'=2] {'seq'}, dimensions={1}, use_global_device_ids=true | all-gather | bytes 589824 | tf_op jit(solution)/shard_map/all_gather | solution.py:87
  71.9 5.1 %copy.23 = bf16[2,256,3,1024]{1,0,3,2:T(2,128)(2,1)S(1)} copy(bf16[2,256,3,1024]{1,3,0,2:T(8,128)(2,1)} %all-gather.11.cloned.1.call-done) | data formatting | bytes 6291456 | tf_op jit(solution)/shard_map/all_gather | solution.py:71
  77.1 2.3 copy.30
  79.3 35.4 %all-gather.13.cloned.1.call-done = bf16[3072,512]{1,0:T(8,128)(2,1)} async-done(((bf16[384,512]{1,0:T(8,128)(2,1)}), bf16[3072,512]{1,0:T(8,128)(2,1)}) %all-gather.13.cloned.1.call-update) | async-done | bytes 3145744 | tf_op jit(solution)/shard_map/all_gather | solution.py:76
  114.7 4.6 %fusion.59 = f32[512,512]{1,0:T(8,128)S(1)} fusion(bf16[512,3072]{0,1:T(8,128)(2,1)} %bitcast.61, bf16[3072,512]{1,0:T(8,128)(2,1)} %all-gather.13.cloned.1.call-done), kind=kOutput, calls=%fused_computation.96 | convolution fusion | flops 1610612736 | bytes 7340032 | tf_op jit(solution)/shard_map/dot_general | solution.py:77
  119.4 0.1 fusion.47
  119.6 2.2 all_gather.40
  121.7 0.5 fusion.26
  122.2 0.2 fusion.18
  122.4 1.8 all-gather.5
  124.2 0.2 fusion.28
  124.5 0.1 fusion.52
  124.6 2.5 %collective-permute-start.3 = (bf16[2,256,512]{1,2,0:T(8,128)(2,1)S(1)}, bf16[2,256,512]{1,2,0:T(8,128)(2,1)S(1)}, u32[]{:S(2)}, u32[]{:S(2)}) collective-permute-start(bf16[2,256,512]{1,2,0:T(8,128)(2,1)S(1)} %get-tuple-element.23), channel_id=1, source_target_pairs={{0,2},{2,4},{4,6},{6,8},{8,10},{10,12},{12,14},{1,3},{3,5},{5,7},{... | collective-permute-start | bytes 1572872 | tf_op jit(solution)/shard_map/ppermute | solution.py:23
  127.1 3.4 %collective-permute-start.4 = (bf16[2,256,512]{1,2,0:T(8,128)(2,1)S(1)}, bf16[2,256,512]{1,2,0:T(8,128)(2,1)S(1)}, u32[]{:S(2)}, u32[]{:S(2)}) collective-permute-start(bf16[2,256,512]{1,2,0:T(8,128)(2,1)S(1)} %get-tuple-element.23), channel_id=1, source_target_pairs={{0,4},{2,6},{4,8},{6,10},{8,12},{10,14},{1,5},{3,7},{5,9},{7,11},{... | collective-permute-start | bytes 1572872 | tf_op jit(solution)/shard_map/ppermute | solution.py:23
  130.4 8.1 %collective-permute-done.3 = bf16[2,256,512]{1,2,0:T(8,128)(2,1)S(1)} collective-permute-done((bf16[2,256,512]{1,2,0:T(8,128)(2,1)S(1)}, bf16[2,256,512]{1,2,0:T(8,128)(2,1)S(1)}, u32[]{:S(2)}, u32[]{:S(2)}) %collective-permute-start.3) | collective-permute-done | bytes 524320 | tf_op jit(solution)/shard_map/ppermute | solution.py:23
  138.6 3.1 %collective-permute-done.4 = bf16[2,256,512]{1,2,0:T(8,128)(2,1)S(1)} collective-permute-done((bf16[2,256,512]{1,2,0:T(8,128)(2,1)S(1)}, bf16[2,256,512]{1,2,0:T(8,128)(2,1)S(1)}, u32[]{:S(2)}, u32[]{:S(2)}) %collective-permute-start.4) | collective-permute-done | bytes 524320 | tf_op jit(solution)/shard_map/ppermute | solution.py:23
  141.6 1.3 pad_maximum_fusion.1
  143.0 0.0 all-gather.17.cloned.1.call-start
  143.0 0.8 copy.33
  143.9 42.6 %all-gather.3 = bf16[1,512,512]{2,1,0:T(8,128)(2,1)} all-gather(bf16[1,64,512]{2,1,0:T(8,128)(2,1)S(1)} %get-tuple-element.32), channel_id=5, replica_groups=mesh['groups'=2,'seq'=8,'chan'=2] {'seq'}, dimensions={1}, use_global_device_ids=true | all-gather | bytes 589824 | tf_op jit(solution)/shard_map/all_gather | solution.py:87
  186.5 5.1 %copy.24 = bf16[2,256,3,1024]{1,0,3,2:T(2,128)(2,1)S(1)} copy(bf16[2,256,3,1024]{1,3,0,2:T(8,128)(2,1)} %all-gather.15.cloned.1.call-done) | data formatting | bytes 6291456 | tf_op jit(solution)/shard_map/all_gather | solution.py:71
  191.7 0.7 copy.32
  192.3 36.8 %all-gather.17.cloned.1.call-done = bf16[3072,512]{1,0:T(8,128)(2,1)} async-done(((bf16[384,512]{1,0:T(8,128)(2,1)}), bf16[3072,512]{1,0:T(8,128)(2,1)}) %all-gather.17.cloned.1.call-update) | async-done | bytes 3145744 | tf_op jit(solution)/shard_map/all_gather | solution.py:76
  229.2 3.8 %fusion.60 = f32[512,512]{1,0:T(8,128)S(1)} fusion(bf16[512,3072]{0,1:T(8,128)(2,1)S(1)} %bitcast.62, bf16[3072,512]{1,0:T(8,128)(2,1)} %all-gather.17.cloned.1.call-done), kind=kOutput, calls=%fused_computation.97 | convolution fusion | flops 1610612736 | bytes 7340032 | tf_op jit(solution)/shard_map/dot_general | solution.py:77
  232.9 0.1 fusion.46
  233.1 2.2 all_gather.46
  235.3 0.5 fusion.24
  235.8 0.1 fusion.7
  235.9 0.8 copy.27
  236.8 0.8 copy.28
  (28 shorter events, 0.2 us)
Async XLA Ops:
  7.2 64.8 %all-gather.11.cloned.1.call-start = ((), (), s32[]{:S(2)}) async-start(), calls=%async_computation | async-start | bytes 4718592 | tf_op jit(solution)/shard_map/all_gather | solution.py:71
  12.6 21.9 %collective-permute-start.2 = (bf16[2,256,512]{1,2,0:T(8,128)(2,1)S(1)}, bf16[2,256,512]{1,2,0:T(8,128)(2,1)S(1)}, u32[]{:S(2)}, u32[]{:S(2)}) collective-permute-start(bf16[2,256,512]{1,2,0:T(8,128)(2,1)S(1)} %get-tuple-element.25), channel_id=1, source_target_pairs={{0,2},{2,4},{4,6},{6,8},{8,10},{10,12},{12,14},{1,3},{3,5},{5,7},{... | collective-permute-start | bytes 1572872 | tf_op jit(solution)/shard_map/ppermute | solution.py:23
  17.4 18.5 %copy-start.3 = (bf16[2,384,2,256]{3,2,1,0:T(2,128)(2,1)S(1)}, bf16[2,384,2,256]{3,2,1,0:T(2,128)(2,1)}, u32[]{:S(2)}) copy-start(bf16[2,384,2,256]{3,2,1,0:T(2,128)(2,1)} %param.8) | copy-start | bytes 2359300
  17.4 17.0 %collective-permute-start = (bf16[2,128,512]{1,2,0:T(8,128)(2,1)S(1)}, bf16[2,128,512]{1,2,0:T(8,128)(2,1)S(1)}, u32[]{:S(2)}, u32[]{:S(2)}) collective-permute-start(bf16[2,128,512]{1,2,0:T(8,128)(2,1)S(1)} %get-tuple-element.26), channel_id=1, source_target_pairs={{0,2},{2,4},{4,6},{6,8},{8,10},{10,12},{12,14},{1,3},{3,5},{5,7},{... | collective-permute-start | bytes 786440 | tf_op jit(solution)/shard_map/ppermute | solution.py:23
  21.0 13.5 %collective-permute-start.1 = (bf16[2,128,512]{1,2,0:T(8,128)(2,1)S(1)}, bf16[2,128,512]{1,2,0:T(8,128)(2,1)S(1)}, u32[]{:S(2)}, u32[]{:S(2)}) collective-permute-start(bf16[2,128,512]{1,2,0:T(8,128)(2,1)S(1)} %get-tuple-element.27), channel_id=1, source_target_pairs={{0,0},{2,2},{4,4},{6,6},{8,8},{10,10},{12,12},{14,14},{1,1},{3,3},... | collective-permute-start | bytes 786440 | tf_op jit(solution)/shard_map/ppermute | solution.py:23
  34.5 2.9 %copy-start.4 = (bf16[2,64,512]{2,1,0:T(8,128)(2,1)S(1)}, bf16[2,64,512]{2,1,0:T(8,128)(2,1)}, u32[]{:S(2)}) copy-start(bf16[2,64,512]{2,1,0:T(8,128)(2,1)} %param.9) | copy-start | bytes 393220
  35.9 78.9 %all-gather.13.cloned.1.call-start = ((), (), s32[]{:S(2)}) async-start(), calls=%async_computation.1 | async-start | bytes 3538944 | tf_op jit(solution)/shard_map/all_gather | solution.py:76
  37.4 149.2 %all-gather.15.cloned.1.call-start = ((), (), s32[]{:S(2)}) async-start(), calls=%async_computation.2 | async-start | bytes 4718592 | tf_op jit(solution)/shard_map/all_gather | solution.py:71
  122.4 20.6 %copy-start = (bf16[256,512]{0,1:T(8,128)(2,1)}, bf16[256,512]{0,1:T(8,128)(2,1)S(1)}, u32[]{:S(2)}) copy-start(bf16[256,512]{0,1:T(8,128)(2,1)S(1)} %get-tuple-element.13) | copy-start | bytes 786436
  124.6 14.0 %collective-permute-start.3 = (bf16[2,256,512]{1,2,0:T(8,128)(2,1)S(1)}, bf16[2,256,512]{1,2,0:T(8,128)(2,1)S(1)}, u32[]{:S(2)}, u32[]{:S(2)}) collective-permute-start(bf16[2,256,512]{1,2,0:T(8,128)(2,1)S(1)} %get-tuple-element.23), channel_id=1, source_target_pairs={{0,2},{2,4},{4,6},{6,8},{8,10},{10,12},{12,14},{1,3},{3,5},{5,7},{... | collective-permute-start | bytes 1572872 | tf_op jit(solution)/shard_map/ppermute | solution.py:23
  127.1 14.6 %collective-permute-start.4 = (bf16[2,256,512]{1,2,0:T(8,128)(2,1)S(1)}, bf16[2,256,512]{1,2,0:T(8,128)(2,1)S(1)}, u32[]{:S(2)}, u32[]{:S(2)}) collective-permute-start(bf16[2,256,512]{1,2,0:T(8,128)(2,1)S(1)} %get-tuple-element.23), channel_id=1, source_target_pairs={{0,4},{2,6},{4,8},{6,10},{8,12},{10,14},{1,5},{3,7},{5,9},{7,11},{... | collective-permute-start | bytes 1572872 | tf_op jit(solution)/shard_map/ppermute | solution.py:23
  143.0 86.2 %all-gather.17.cloned.1.call-start = ((), (), s32[]{:S(2)}) async-start(), calls=%async_computation.3 | async-start | bytes 3538944 | tf_op jit(solution)/shard_map/all_gather | solution.py:76
  229.1 6.1 %copy-start.2 = (bf16[1,512,512]{2,1,0:T(8,128)(2,1)S(1)}, bf16[1,512,512]{2,1,0:T(8,128)(2,1)}, u32[]{:S(2)}) copy-start(bf16[1,512,512]{2,1,0:T(8,128)(2,1)} %all-gather.3) | copy-start | bytes 1572868
  232.9 2.9 %copy-start.1 = (bf16[256,512]{0,1:T(8,128)(2,1)S(1)}, bf16[256,512]{0,1:T(8,128)(2,1)}, u32[]{:S(2)}) copy-start(bf16[256,512]{0,1:T(8,128)(2,1)} %copy-done) | copy-start | bytes 786436
Sparse Core Ops, SparseCore 0:
  36.0 14.3 all-gather.10
  52.6 62.1 all-gather.12
  143.1 21.7 all-gather.14
  166.9 62.1 all-gather.16
